TPU v7x, 128 devices: a whole 4x4x4 slice. The times are simulated.
128 devices in a mesh: dp: 16 (over z, x), tm: 8 (over y, core).
Axes of the slice: x: 4, y: 4, z: 4, core: 2. Of those that a mesh axis runs over, the one named last changes fastest.
Arguments:
- frames: bfloat16 [16, 6144, 1024], P('dp', 'tm'), may hold values from -18 to 18
- lengths: int32 [16], P('dp'), may hold values from 1 to 6144, 58982 in all
- w_in: bfloat16 [1024, 2048], replicated, may hold values from -4 to 4
- w_dw: float32 [31, 1024], replicated, may hold values from -1 to 1
- bn_gain: float32 [1024], replicated, may hold values from 0.25 to 1.75
- bn_bias: float32 [1024], replicated, may hold values from -1 to 1
- w_out: bfloat16 [1024, 1024], replicated, may hold values from -0.1875 to 0.1875
- cotangent: bfloat16 [16, 6144, 1024], P('dp', 'tm'), may hold values from -6 to 6
Outputs:
- output: bfloat16 [16, 6144, 1024], P('dp', 'tm')
- grad_frames: bfloat16 [16, 6144, 1024], P('dp', 'tm')
- grad_w_in: float32 [1024, 2048], P(('dp', 'tm'))
- grad_w_out: float32 [1024, 1024], P(('dp', 'tm'))
- grad_kernel: float32 [31, 1024], replicated
- grad_gain: float32 [1024], replicated
- grad_bias: float32 [1024], replicated
Inputs may be any that keep to these rules, and one draw needn't show every extreme that they name: Frame slots at or after a recording's length are padding; the lengths sum to 58982 and the longest is exactly 6144.
All inputs are finite; a program needn't handle non-finite values. No bound on the sum of `lengths` on one device may be relied on, other than what follows from the above.
Results may differ from a plain program's by a relative error of at most 0.015.
Values may be sent and summed in bfloat16 or wider, within the bound.
A program may use at most 128 MiB of HBM per device.

v0:
```python
import math
import jax
import jax.numpy as jnp
from jax import lax
from jax.sharding import PartitionSpec as P


def padded_2(cells, sides, width):
    for axis, dim in sides:
        count = lax.axis_size(axis)
        ends = count - 1
        head = lax.slice_in_dim(cells, 0, width, axis=dim)
        tail = lax.slice_in_dim(cells, cells.shape[dim] - width, cells.shape[dim], axis=dim)
        cells = jnp.concatenate(
            [
                lax.ppermute(tail, axis, [(i, (i + 1) % count) for i in range(ends)]),
                cells,
                lax.ppermute(head, axis, [((i + 1) % count, i) for i in range(ends)]),
            ],
            axis=dim,
        )
    return cells


def taps_forward(padded, kernel, frame_count):
    summed = jnp.zeros((frame_count, padded.shape[1]), jnp.float32)
    for tap_index in range(kernel.shape[0]):
        summed = summed + kernel[tap_index] * padded[tap_index : tap_index + frame_count].astype(
            jnp.float32
        )
    return summed


def taps_backward(padded_grad, kernel, frame_count):
    reach_both = kernel.shape[0] - 1
    summed = jnp.zeros((frame_count, padded_grad.shape[1]), jnp.float32)
    for tap_index in range(kernel.shape[0]):
        begin = reach_both - tap_index
        summed = summed + kernel[tap_index] * padded_grad[begin : begin + frame_count].astype(
            jnp.float32
        )
    return summed


def taps_kernel(padded_glu, dconv_rows, kernel_taps, frame_count):
    grad_rows = dconv_rows.astype(jnp.float32)
    tap_rows = []
    for tap_index in range(kernel_taps):
        tap_rows.append(
            jnp.sum(
                padded_glu[tap_index : tap_index + frame_count].astype(jnp.float32) * grad_rows,
                axis=0,
            )
        )
    return jnp.stack(tap_rows)


def row_product(left_rows, right_mat, contract):
    dim_spec = (((1,), (contract,)), ((), ()))
    return lax.dot_general(left_rows, right_mat, dim_spec, preferred_element_type=jnp.float32)


def local(frames, lengths, w_in, w_dw, bn_gain, bn_bias, w_out, cotangent):
    frame_rows = frames.shape[1]
    channels = frames.shape[2]
    kernel_taps = w_dw.shape[0]
    reach = (kernel_taps - 1) // 2
    feats = frames[0]
    cot_rows = cotangent[0]
    tm_count = lax.axis_size("tm")
    device_count = lax.axis_size("dp") * tm_count
    offset = lax.axis_index("tm") * frame_rows
    limit = lengths[0]
    positions = offset + jnp.arange(frame_rows, dtype=jnp.int32)
    live_rows = (positions < limit).astype(jnp.float32)[:, None]
    contract_frames = (((0,), (0,)), ((), ()))
    pre_act = row_product(feats, w_in, 0)
    linear_half = pre_act[:, :channels]
    gate_sig = jax.nn.sigmoid(pre_act[:, channels:])
    glu_out = (linear_half * gate_sig * live_rows).astype(jnp.bfloat16)
    dswish = row_product(cot_rows, w_out, 1)
    padded = padded_2(glu_out, (("tm", 0),), reach)
    conv_out = taps_forward(padded, w_dw, frame_rows)
    local_sum = jnp.sum(conv_out * live_rows, axis=0)
    local_sq = jnp.sum(conv_out * conv_out * live_rows, axis=0)
    local_count = jnp.sum(live_rows)
    sums, squares, count = lax.psum((local_sum, local_sq, local_count), ("dp", "tm"))
    mean_vec = sums / count
    variance = squares / count - mean_vec * mean_vec
    inv_std = lax.rsqrt(variance + 1e-05)
    normed = (conv_out - mean_vec) * inv_std
    shifted = bn_gain * normed + bn_bias
    act_sig = jax.nn.sigmoid(shifted)
    swished = (shifted * act_sig * live_rows).astype(jnp.bfloat16)
    dshift = live_rows * dswish * act_sig * (1.0 + shifted * (1.0 - act_sig))
    sum_gain, sum_bias = lax.psum(
        (jnp.sum(dshift * normed, axis=0), jnp.sum(dshift, axis=0)), ("dp", "tm")
    )
    dconv = (
        live_rows * bn_gain * inv_std * (dshift - sum_bias / count - normed * sum_gain / count)
    ).astype(jnp.bfloat16)
    padded_grad = padded_2(dconv, (("tm", 0),), reach)
    dglu = live_rows * taps_backward(padded_grad, w_dw, frame_rows)
    kernel_sum = lax.psum(taps_kernel(padded, dconv, kernel_taps, frame_rows), ("dp", "tm"))
    out_rows = row_product(swished, w_out, 0).astype(jnp.bfloat16)
    dpre = jnp.concatenate(
        [dglu * gate_sig, dglu * linear_half * gate_sig * (1.0 - gate_sig)], axis=1
    ).astype(jnp.bfloat16)
    grad_rows = row_product(dpre, w_in, 1).astype(jnp.bfloat16)
    term_in = lax.dot_general(feats, dpre, contract_frames, preferred_element_type=jnp.float32)
    term_out = lax.dot_general(
        swished, cot_rows, contract_frames, preferred_element_type=jnp.float32
    )
    weight_term = jnp.concatenate([term_in, term_out], axis=1)
    weight_sum = lax.psum_scatter(weight_term, ("dp", "tm"), scatter_dimension=0, tiled=True)
    scale = 1.0 / math.sqrt(device_count * frame_rows)
    grad_w_in = weight_sum[:, : 2 * channels] * scale
    grad_w_out = weight_sum[:, 2 * channels :] * scale
    return (
        out_rows[None],
        grad_rows[None],
        grad_w_in,
        grad_w_out,
        kernel_sum * scale,
        sum_gain * scale,
        sum_bias * scale,
    )


def solution(mesh):
    placed = (P("dp", "tm", None), P("dp"), P(), P(), P(), P(), P(), P("dp", "tm", None))
    return jax.shard_map(
        local,
        mesh=mesh,
        in_specs=placed,
        out_specs=(
            P("dp", "tm", None),
            P("dp", "tm", None),
            P(("dp", "tm"), None),
            P(("dp", "tm"), None),
            P(),
            P(),
            P(),
        ),
        check_vma=False,
    )
```

profile of v0, /device:TPU:0, one launch (start us, length us, event | category | flops | bytes accessed | tf_op | source)
XLA Modules:
  0.0 603.7 jit_solution(6638876811179374699)
XLA Ops:
  8.0 5.7 fusion.143
  19.8 3.0 collective-permute-done.1
  22.8 24.4 %multiply_reduce_fusion.2 = (f32[1024]{0:T(1024)S(1)}, f32[1024]{0:T(1024)S(1)}, f32[768,1024]{1,0:T(8,128)}) fusion(f32[768]{0:T(1024)S(1)} %fusion.147, bf16[15,1024]{1,0:T(8,128)(2,1)S(1)} %collective-permute-done.1, bf16[768,1024]{1,0:T(8,128)(2,1)S(1)} %multiply_convert_fusion.4, f32[1024]{0:T(1024)S(1)} %bitcast.146, f32[1024]{0:T(1024)S(1)} %bitcast.148, ...), kind=kLoop, calls=%fused_computation.213 | loop fusion | flops 147060736 | bytes 4918272 | tf_op jit(solution)/shard_map/reduce_sum | solution.py:84
  47.2 69.6 %all-reduce.1 = (f32[1024]{0:T(1024)S(1)}, f32[]{:T(128)}, f32[1024]{0:T(1024)S(1)}) all-reduce(f32[1024]{0:T(1024)S(1)} %get-tuple-element.52, f32[]{:T(128)} %fusion.148, f32[1024]{0:T(1024)S(1)} %get-tuple-element.51), channel_id=1, replica_groups=mesh['dp'=16,'tm'=8] {'dp','tm'}, use_global_device_ids=true, to_apply=%region_5.0 | all-reduce | flops 2049 | bytes 16392 | tf_op jit(solution)/shard_map/psum | solution.py:87
  117.6 6.4 %fusion.151 = (f32[1024]{0:T(1024)S(1)}, f32[1024]{0:T(1024)S(1)}, f32[768,1024]{1,0:T(8,128)}) fusion(f32[1024]{0:T(1024)S(1)} %get-tuple-element.106, f32[768,1024]{1,0:T(8,128)} %get-tuple-element.67, f32[1024]{0:T(1024)S(1)} %get-tuple-element.105, f32[1024]{0:T(1024)S(1)} %copy-done.16, f32[1024]{0:T(1024)S(1)} %copy-done.12, ...), kind=kOutput, calls=%fused_computation.316 | convolution fusion | flops 1623193600 | bytes 9989120 | tf_op jit(solution)/shard_map/dot_general | solution.py:60
  124.0 63.8 %all-reduce = (f32[1024]{0:T(1024)S(1)}, f32[1024]{0:T(1024)S(1)}) all-reduce(f32[1024]{0:T(1024)S(1)} %get-tuple-element.58, f32[1024]{0:T(1024)S(1)} %get-tuple-element.57), channel_id=1, replica_groups=mesh['dp'=16,'tm'=8] {'dp','tm'}, use_global_device_ids=true, to_apply=%region_9.0 | all-reduce | flops 2048 | bytes 16384 | tf_op jit(solution)/shard_map/psum | solution.py:96
  189.0 15.0 %fusion.75 = (f32[1024]{0:T(1024)S(1)}, f32[1024]{0:T(1024)S(1)}, f32[1024]{0:T(1024)S(1)}, f32[1024]{0:T(1024)S(1)}, f32[1024]{0:T(1024)S(1)}, /*index=5*/f32[1024]{0:T(1024)S(1)}, bf16[768,1024]{1,0:T(8,128)(2,1)S(1)}) fusion(bf16[15,1024]{1,0:T(8,128)(2,1)S(1)} %collective-permute-done.1, bf16[768,1024]{1,0:T(8,128)(2,1)} %copy-done.1, ...), kind=kLoop, calls=%fused_computation.196 | loop fusion | flops 36956160 | bytes 9516036 | tf_op jit(solution)/shard_map/reduce_sum | solution.py:50
  205.4 3.0 collective-permute-start.3
  208.4 2.7 fusion.60
  211.1 3.2 fusion.74
  214.4 2.9 fusion.59
  217.3 3.7 fusion.76
  221.0 4.5 fusion.139
  225.5 2.7 stack.127
  228.2 40.0 %multiply_convert_fusion.1 = (bf16[768,1024]{1,0:T(8,128)(2,1)S(1)}, f32[768,1024]{1,0:T(8,128)S(1)}) fusion(f32[768,2048]{1,0:T(8,128)} %copy-done.4, bf16[768,1024]{1,0:T(8,128)(2,1)} %copy-done.3, bf16[15,1024]{1,0:T(8,128)(2,1)S(1)} %collective-permute-done.3, f32[1024]{0:T(1024)S(1)} %bitcast.147, f32[1024]{0:T(1024)S(1)} %bitcast.149, ...), kind=kLoop, calls=%fused_computation.204 | loop fusion | flops 147849216 | bytes 9628672 | tf_op jit(solution)/shard_map/convert
  268.2 4.7 multiply_convert_fusion
  273.0 3.5 convolution_bitcast_fusion
  276.5 8.0 %pad_maximum_fusion = f32[1024,3072]{0,1:T(8,128)} fusion(f32[1024,1024]{0,1:T(8,128)S(1)} %copy-done.6, f32[1024,2048]{0,1:T(8,128)S(1)} %convolution_bitcast_fusion), kind=kLoop, calls=%fused_computation.32 | loop fusion | flops 3145728 | bytes 25165824 | tf_op jit(solution)/shard_map/concatenate | solution.py:114
  284.5 12.6 %copy.19 = f32[1024,3072]{1,0:T(8,128)} copy(f32[1024,3072]{0,1:T(8,128)} %pad_maximum_fusion) | data formatting | bytes 25165824
  297.7 5.4 fusion.146
  303.1 4.6 fusion.145
  307.6 58.1 %all-reduce.4.cloned.1.call-done = f32[31,1024]{1,0:T(8,128)} async-done(((f32[31,1024]{1,0:T(8,128)}), f32[31,1024]{1,0:T(8,128)}) %all-reduce.4.cloned.1.call-update) | async-done | bytes 126992 | tf_op jit(solution)/shard_map/psum | solution.py:104
  367.4 223.3 %reduce-scatter.4.cloned.1.call-done = f32[8,3072]{1,0:T(8,128)} async-done(((f32[1024,3072]{1,0:T(8,128)}), f32[8,3072]{1,0:T(8,128)}) %reduce-scatter.4.cloned.1.call-update) | async-done | bytes 98320
  594.7 2.2 copy.17
  (62 shorter events, 15.7 us)
Async XLA Ops:
  7.2 110.4 %copy-start = (bf16[1024,1024]{1,0:T(8,128)(2,1)S(1)}, bf16[1024,1024]{1,0:T(8,128)(2,1)}, u32[]{:S(2)}) copy-start(bf16[1024,1024]{1,0:T(8,128)(2,1)} %param.14) | copy-start | bytes 6291460
  7.2 358.6 %all-reduce.4.cloned.1.call-start = ((), (), s32[]{:S(2)}) async-start(), calls=%async_computation.1 | async-start | bytes 262144 | tf_op jit(solution)/shard_map/psum | solution.py:104
  13.7 2.7 copy-start.4
  13.7 5.4 copy-start.11
  16.4 6.4 %copy-start.1 = (bf16[768,1024]{1,0:T(8,128)(2,1)}, bf16[768,1024]{1,0:T(8,128)(2,1)S(1)}, u32[]{:S(2)}) copy-start(bf16[768,1024]{1,0:T(8,128)(2,1)S(1)} %multiply_convert_fusion.4) | copy-start | bytes 4718596
  16.4 101.2 %copy-start.12 = (f32[1024]{0:T(1024)S(1)}, f32[1024]{0:T(1024)}, u32[]{:S(2)}) copy-start(f32[1024]{0:T(1024)} %param.12) | copy-start | bytes 12292
  16.4 101.2 %copy-start.16 = (f32[1024]{0:T(1024)S(1)}, f32[1024]{0:T(1024)}, u32[]{:S(2)}) copy-start(f32[1024]{0:T(1024)} %param.13) | copy-start | bytes 12292
  16.4 3.5 collective-permute-start
  17.8 5.0 collective-permute-start.1
  189.0 19.4 %copy-start.2 = (bf16[768,1024]{1,0:T(8,128)(2,1)S(1)}, bf16[768,1024]{1,0:T(8,128)(2,1)}, u32[]{:S(2)}) copy-start(bf16[768,1024]{1,0:T(8,128)(2,1)} %copy-done.1) | copy-start | bytes 4718596
  204.0 13.2 %copy-start.3 = (bf16[768,1024]{1,0:T(8,128)(2,1)}, bf16[768,1024]{1,0:T(8,128)(2,1)S(1)}, u32[]{:S(2)}) copy-start(bf16[768,1024]{1,0:T(8,128)(2,1)S(1)} %get-tuple-element.64) | copy-start | bytes 4718596
  204.1 24.1 %collective-permute-start.2 = (bf16[15,1024]{1,0:T(8,128)(2,1)S(1)}, bf16[15,1024]{1,0:T(8,128)(2,1)S(1)}, u32[]{:S(2)}, u32[]{:S(2)}) collective-permute-start(bf16[15,1024]{1,0:T(8,128)(2,1)S(1)} %get-tuple-element.68), channel_id=1, source_target_pairs={{1,0},{2,1},{3,2},{4,3},{5,4},{6,5},{7,6},{9,8},{10,9},{11,10},{12... | collective-permute-start | bytes 92168 | tf_op jit(solution)/shard_map/ppermute | solution.py:18
  205.4 22.8 %collective-permute-start.3 = (bf16[15,1024]{1,0:T(8,128)(2,1)S(1)}, bf16[15,1024]{1,0:T(8,128)(2,1)S(1)}, u32[]{:S(2)}, u32[]{:S(2)}) collective-permute-start(bf16[15,1024]{1,0:T(8,128)(2,1)S(1)} %get-tuple-element.69), channel_id=1, source_target_pairs={{0,1},{1,2},{2,3},{3,4},{4,5},{5,6},{6,7},{8,9},{9,10},{10,11},{11... | collective-permute-start | bytes 92168 | tf_op jit(solution)/shard_map/ppermute | solution.py:16
  214.3 6.6 %copy-start.5 = (f32[768,1024]{1,0:T(8,128)S(1)}, f32[768,1024]{1,0:T(8,128)}, u32[]{:S(2)}) copy-start(f32[768,1024]{1,0:T(8,128)} %get-tuple-element.67) | copy-start | bytes 9437188
  214.3 6.6 %copy-start.14 = (bf16[1,768,1024]{2,1,0:T(8,128)(2,1)S(1)}, bf16[1,768,1024]{2,1,0:T(8,128)(2,1)}, u32[]{:S(2)}) copy-start(bf16[1,768,1024]{2,1,0:T(8,128)(2,1)} %param.15) | copy-start | bytes 4718596
  228.1 362.5 %reduce-scatter.4.cloned.1.call-start = ((), (), s32[]{:S(2)}) async-start(), calls=%async_computation.2 | async-start | bytes 12681216
  268.2 4.7 copy-start.7
  268.2 4.7 copy-start.15
  272.9 3.5 copy-start.9
  272.9 3.5 copy-start.6
  297.7 5.4 copy-start.8
  297.7 5.4 copy-start.10
  297.7 5.4 copy-start.13
Sparse Core Ops, SparseCore 0:
  228.3 137.4 all-reduce.3
  371.5 219.0 reduce-scatter.3
where the time goes:
time: 604 us
  waiting for transfers between devices  284 us (47%)
  blocking collectives  133 us (22%)
  other arithmetic  111 us (18%)
  matrix products  30 us (5%)
  local copies, waits for them, and re-layouts  22.3 us (4%)
  between operations  15.2 us (3%)
  starting transfers between devices  7.12 us (1%)
    unnamed x3, waiting for transfers between devices  223 us
    psum x1, blocking collectives, local(): lax.psum((local_sum, local_sq, local_count), ('dp', 'tm'))  69.6 us
    psum x1, blocking collectives, local(): lax.psum((jnp.sum(dshift * normed, axis=0), jnp.sum(dshift, axis=0)), ('d...  63.8 us
    psum x1, waiting for transfers between devices, local(): lax.psum(taps_kernel(padded, dconv, kernel_taps, frame_rows), ('dp', 'tm'))  58.1 us
    another operation x2, other arithmetic  44.7 us
    reduce_sum x5, other arithmetic, taps_kernel(): jnp.sum(padded_glu[tap_index:tap_index + frame_count].astype(jnp.float32)...  27.5 us
    reduce_sum x1, other arithmetic, local(): local_sum = jnp.sum(conv_out * live_rows, axis=0)  24.4 us
    dot_general x4, matrix products, row_product(): lax.dot_general(left_rows, right_mat, dim_spec, preferred_element_type=jn...  22 us
  transfers between devices with their start and end apart: 6, of which 3 were waited for; matrix products, arithmetic and copies ran while one was open for 17% of the time, Pallas kernels for 0%

commit v1 on v0

--- a/solution.py
+++ b/solution.py
@@ -94,7 +94,7 @@
     swished = (shifted * act_sig * live_rows).astype(jnp.bfloat16)
     dshift = live_rows * dswish * act_sig * (1.0 + shifted * (1.0 - act_sig))
     sum_gain, sum_bias = lax.psum(
-        (jnp.sum(dshift * normed, axis=0), jnp.sum(dshift, axis=0)), ("dp", "tm")
+        lax.psum((jnp.sum(dshift * normed, axis=0), jnp.sum(dshift, axis=0)), "tm"), "dp"
     )
     dconv = (
         live_rows * bn_gain * inv_std * (dshift - sum_bias / count - normed * sum_gain / count)

time: 604 us -> 589 us (0.975)
  blocking collectives: 133 us -> 122 us
    psum x1 -> x2, blocking collectives: 63.8 us -> 52.6 us  [the longest x1 38.8 us: local(): lax.psum(lax.psum((jnp.sum(dshift * normed, axis=0), jnp.sum(dshift, axis...]
where the time goes in v1:
time: 589 us
  waiting for transfers between devices  281 us (48%)
  blocking collectives  122 us (21%)
  other arithmetic  111 us (19%)
  matrix products  30 us (5%)
  local copies, waits for them, and re-layouts  22.3 us (4%)
  between operations  15.2 us (3%)
  starting transfers between devices  7.12 us (1%)
    unnamed x3, waiting for transfers between devices  223 us
    psum x1, blocking collectives, local(): lax.psum((local_sum, local_sq, local_count), ('dp', 'tm'))  69.6 us
    psum x1, waiting for transfers between devices, local(): lax.psum(taps_kernel(padded, dconv, kernel_taps, frame_rows), ('dp', 'tm'))  54.2 us
    another operation x2, other arithmetic  44.7 us
    psum x1, blocking collectives, local(): lax.psum(lax.psum((jnp.sum(dshift * normed, axis=0), jnp.sum(dshift, axis...  38.8 us
    reduce_sum x5, other arithmetic, taps_kernel(): jnp.sum(padded_glu[tap_index:tap_index + frame_count].astype(jnp.float32)...  27.5 us
    reduce_sum x1, other arithmetic, local(): local_sum = jnp.sum(conv_out * live_rows, axis=0)  24.4 us
    dot_general x4, matrix products, row_product(): lax.dot_general(left_rows, right_mat, dim_spec, preferred_element_type=jn...  22 us
  transfers between devices with their start and end apart: 6, of which 3 were waited for; matrix products, arithmetic and copies ran while one was open for 17% of the time, Pallas kernels for 0%

profile of v1, /device:TPU:0, one launch (start us, length us, event | category | flops | bytes accessed | tf_op | source)
XLA Modules:
  0.0 588.6 jit_solution(4118596936792861598)
XLA Ops:
  8.0 5.7 fusion.143
  19.8 3.0 collective-permute-done.1
  22.8 24.4 %multiply_reduce_fusion.2 = (f32[1024]{0:T(1024)S(1)}, f32[1024]{0:T(1024)S(1)}, f32[768,1024]{1,0:T(8,128)}) fusion(f32[768]{0:T(1024)S(1)} %fusion.147, bf16[15,1024]{1,0:T(8,128)(2,1)S(1)} %collective-permute-done.1, bf16[768,1024]{1,0:T(8,128)(2,1)S(1)} %multiply_convert_fusion.4, f32[1024]{0:T(1024)S(1)} %bitcast.146, f32[1024]{0:T(1024)S(1)} %bitcast.148, ...), kind=kLoop, calls=%fused_computation.213 | loop fusion | flops 147060736 | bytes 4918272 | tf_op jit(solution)/shard_map/reduce_sum | solution.py:84
  47.2 69.6 %all-reduce = (f32[1024]{0:T(1024)S(1)}, f32[]{:T(128)}, f32[1024]{0:T(1024)S(1)}) all-reduce(f32[1024]{0:T(1024)S(1)} %get-tuple-element.52, f32[]{:T(128)} %fusion.148, f32[1024]{0:T(1024)S(1)} %get-tuple-element.51), channel_id=1, replica_groups=mesh['dp'=16,'tm'=8] {'dp','tm'}, use_global_device_ids=true, to_apply=%region_5.0 | all-reduce | flops 2049 | bytes 16392 | tf_op jit(solution)/shard_map/psum | solution.py:87
  117.5 6.4 %fusion.151 = (f32[1024]{0:T(1024)S(1)}, f32[1024]{0:T(1024)S(1)}, f32[768,1024]{1,0:T(8,128)}) fusion(f32[1024]{0:T(1024)S(1)} %get-tuple-element.108, f32[768,1024]{1,0:T(8,128)} %get-tuple-element.69, f32[1024]{0:T(1024)S(1)} %get-tuple-element.107, f32[1024]{0:T(1024)S(1)} %copy-done.16, f32[1024]{0:T(1024)S(1)} %copy-done.12, ...), kind=kOutput, calls=%fused_computation.316 | convolution fusion | flops 1623193600 | bytes 9989120 | tf_op jit(solution)/shard_map/dot_general | solution.py:60
  124.0 13.8 %all-reduce.2 = (f32[1024]{0:T(1024)S(1)}, f32[1024]{0:T(1024)S(1)}) all-reduce(f32[1024]{0:T(1024)S(1)} %get-tuple-element.58, f32[1024]{0:T(1024)S(1)} %get-tuple-element.57), channel_id=1, replica_groups=mesh['dp'=16,'tm'=8] {'tm'}, use_global_device_ids=true, to_apply=%region_10.0 | all-reduce | flops 2048 | bytes 16384 | tf_op jit(solution)/shard_map/psum | solution.py:97
  137.8 38.8 %all-reduce.1 = (f32[1024]{0:T(1024)S(1)}, f32[1024]{0:T(1024)S(1)}) all-reduce(f32[1024]{0:T(1024)S(1)} %get-tuple-element.64, f32[1024]{0:T(1024)S(1)} %get-tuple-element.65), channel_id=1, replica_groups=mesh['dp'=16,'tm'=8] {'dp'}, use_global_device_ids=true, to_apply=%region_11.0 | all-reduce | flops 2048 | bytes 16384 | tf_op jit(solution)/shard_map/psum | solution.py:96
  177.8 15.0 %fusion.75 = (f32[1024]{0:T(1024)S(1)}, f32[1024]{0:T(1024)S(1)}, f32[1024]{0:T(1024)S(1)}, f32[1024]{0:T(1024)S(1)}, f32[1024]{0:T(1024)S(1)}, /*index=5*/f32[1024]{0:T(1024)S(1)}, bf16[768,1024]{1,0:T(8,128)(2,1)S(1)}) fusion(bf16[15,1024]{1,0:T(8,128)(2,1)S(1)} %collective-permute-done.1, bf16[768,1024]{1,0:T(8,128)(2,1)} %copy-done.1, ...), kind=kLoop, calls=%fused_computation.196 | loop fusion | flops 36956160 | bytes 9516036 | tf_op jit(solution)/shard_map/reduce_sum | solution.py:50
  194.2 3.0 collective-permute-start.3
  197.2 2.7 fusion.60
  199.9 3.2 fusion.74
  203.2 2.9 fusion.59
  206.1 3.7 fusion.76
  209.8 4.5 fusion.139
  214.3 2.7 stack.127
  217.0 40.0 %multiply_convert_fusion.1 = (bf16[768,1024]{1,0:T(8,128)(2,1)S(1)}, f32[768,1024]{1,0:T(8,128)S(1)}) fusion(f32[768,2048]{1,0:T(8,128)} %copy-done.4, bf16[768,1024]{1,0:T(8,128)(2,1)} %copy-done.3, bf16[15,1024]{1,0:T(8,128)(2,1)S(1)} %collective-permute-done.3, f32[1024]{0:T(1024)S(1)} %bitcast.147, f32[1024]{0:T(1024)S(1)} %bitcast.149, ...), kind=kLoop, calls=%fused_computation.204 | loop fusion | flops 147849216 | bytes 9628672 | tf_op jit(solution)/shard_map/convert
  257.0 4.7 multiply_convert_fusion
  261.8 3.5 convolution_bitcast_fusion
  265.3 8.0 %pad_maximum_fusion = f32[1024,3072]{0,1:T(8,128)} fusion(f32[1024,1024]{0,1:T(8,128)S(1)} %copy-done.6, f32[1024,2048]{0,1:T(8,128)S(1)} %convolution_bitcast_fusion), kind=kLoop, calls=%fused_computation.32 | loop fusion | flops 3145728 | bytes 25165824 | tf_op jit(solution)/shard_map/concatenate | solution.py:114
  273.3 12.6 %copy.19 = f32[1024,3072]{1,0:T(8,128)} copy(f32[1024,3072]{0,1:T(8,128)} %pad_maximum_fusion) | data formatting | bytes 25165824
  286.5 5.4 fusion.146
  291.9 4.6 fusion.145
  296.5 54.2 %all-reduce.5.cloned.1.call-done = f32[31,1024]{1,0:T(8,128)} async-done(((f32[31,1024]{1,0:T(8,128)}), f32[31,1024]{1,0:T(8,128)}) %all-reduce.5.cloned.1.call-update) | async-done | bytes 126992 | tf_op jit(solution)/shard_map/psum | solution.py:104
  352.3 223.3 %reduce-scatter.4.cloned.1.call-done = f32[8,3072]{1,0:T(8,128)} async-done(((f32[1024,3072]{1,0:T(8,128)}), f32[8,3072]{1,0:T(8,128)}) %reduce-scatter.4.cloned.1.call-update) | async-done | bytes 98320
  (63 shorter events, 17.8 us)
Async XLA Ops:
  7.2 110.4 %copy-start = (bf16[1024,1024]{1,0:T(8,128)(2,1)S(1)}, bf16[1024,1024]{1,0:T(8,128)(2,1)}, u32[]{:S(2)}) copy-start(bf16[1024,1024]{1,0:T(8,128)(2,1)} %param.14) | copy-start | bytes 6291460
  7.2 343.5 %all-reduce.5.cloned.1.call-start = ((), (), s32[]{:S(2)}) async-start(), calls=%async_computation.1 | async-start | bytes 262144 | tf_op jit(solution)/shard_map/psum | solution.py:104
  13.7 2.7 copy-start.4
  13.7 5.4 copy-start.11
  16.4 6.4 %copy-start.1 = (bf16[768,1024]{1,0:T(8,128)(2,1)}, bf16[768,1024]{1,0:T(8,128)(2,1)S(1)}, u32[]{:S(2)}) copy-start(bf16[768,1024]{1,0:T(8,128)(2,1)S(1)} %multiply_convert_fusion.4) | copy-start | bytes 4718596
  16.4 101.2 %copy-start.12 = (f32[1024]{0:T(1024)S(1)}, f32[1024]{0:T(1024)}, u32[]{:S(2)}) copy-start(f32[1024]{0:T(1024)} %param.12) | copy-start | bytes 12292
  16.4 101.2 %copy-start.16 = (f32[1024]{0:T(1024)S(1)}, f32[1024]{0:T(1024)}, u32[]{:S(2)}) copy-start(f32[1024]{0:T(1024)} %param.13) | copy-start | bytes 12292
  16.4 3.5 collective-permute-start
  17.8 5.0 collective-permute-start.1
  177.8 19.4 %copy-start.2 = (bf16[768,1024]{1,0:T(8,128)(2,1)S(1)}, bf16[768,1024]{1,0:T(8,128)(2,1)}, u32[]{:S(2)}) copy-start(bf16[768,1024]{1,0:T(8,128)(2,1)} %copy-done.1) | copy-start | bytes 4718596
  192.9 13.2 %copy-start.3 = (bf16[768,1024]{1,0:T(8,128)(2,1)}, bf16[768,1024]{1,0:T(8,128)(2,1)S(1)}, u32[]{:S(2)}) copy-start(bf16[768,1024]{1,0:T(8,128)(2,1)S(1)} %get-tuple-element.66) | copy-start | bytes 4718596
  192.9 24.1 %collective-permute-start.2 = (bf16[15,1024]{1,0:T(8,128)(2,1)S(1)}, bf16[15,1024]{1,0:T(8,128)(2,1)S(1)}, u32[]{:S(2)}, u32[]{:S(2)}) collective-permute-start(bf16[15,1024]{1,0:T(8,128)(2,1)S(1)} %get-tuple-element.70), channel_id=1, source_target_pairs={{1,0},{2,1},{3,2},{4,3},{5,4},{6,5},{7,6},{9,8},{10,9},{11,10},{12... | collective-permute-start | bytes 92168 | tf_op jit(solution)/shard_map/ppermute | solution.py:18
  194.2 22.8 %collective-permute-start.3 = (bf16[15,1024]{1,0:T(8,128)(2,1)S(1)}, bf16[15,1024]{1,0:T(8,128)(2,1)S(1)}, u32[]{:S(2)}, u32[]{:S(2)}) collective-permute-start(bf16[15,1024]{1,0:T(8,128)(2,1)S(1)} %get-tuple-element.71), channel_id=1, source_target_pairs={{0,1},{1,2},{2,3},{3,4},{4,5},{5,6},{6,7},{8,9},{9,10},{10,11},{11... | collective-permute-start | bytes 92168 | tf_op jit(solution)/shard_map/ppermute | solution.py:16
  203.1 6.6 %copy-start.5 = (f32[768,1024]{1,0:T(8,128)S(1)}, f32[768,1024]{1,0:T(8,128)}, u32[]{:S(2)}) copy-start(f32[768,1024]{1,0:T(8,128)} %get-tuple-element.69) | copy-start | bytes 9437188
  203.1 6.6 %copy-start.14 = (bf16[1,768,1024]{2,1,0:T(8,128)(2,1)S(1)}, bf16[1,768,1024]{2,1,0:T(8,128)(2,1)}, u32[]{:S(2)}) copy-start(bf16[1,768,1024]{2,1,0:T(8,128)(2,1)} %param.15) | copy-start | bytes 4718596
  216.9 358.6 %reduce-scatter.4.cloned.1.call-start = ((), (), s32[]{:S(2)}) async-start(), calls=%async_computation.2 | async-start | bytes 12681216
  257.0 4.7 copy-start.7
  257.0 4.7 copy-start.15
  261.7 3.5 copy-start.9
  261.7 3.5 copy-start.6
  286.5 5.4 copy-start.8
  286.5 5.4 copy-start.10
  286.5 5.4 copy-start.13
Sparse Core Ops, SparseCore 0:
  217.1 133.5 all-reduce.4
  356.4 219.0 reduce-scatter.3
